TPU v7x, 32 devices: a whole 2x2x4 slice. The times are simulated.
32 devices in a mesh: parts: 2 (over x), blk: 16 (over z, y, core).
Axes of the slice: x: 2, y: 2, z: 4, core: 2. Of those that a mesh axis runs over, the one named last changes fastest.
Arguments:
- activations: bfloat16 [32, 160, 4096], P(('parts', 'blk')), parts along dimension 0, may hold values from -6 to 6
- output_grads: bfloat16 [32, 160, 14336], P(('parts', 'blk')), parts along dimension 0, may hold values from -6 to 6
- basis_in: bfloat16 [4096, 4096], P('blk'), may hold values from -0.09375 to 0.09375
- basis_out: bfloat16 [14336, 14336], P('blk'), may hold values from -0.046875 to 0.046875
- query_left: bfloat16 [16, 32, 4096], P('blk'), may hold values from -0.09375 to 0.09375
- query_right: bfloat16 [16, 32, 14336], P('blk'), may hold values from -0.046875 to 0.046875
- owners: int32 [4], replicated, may hold values from 0 to 15, as said below
- lengths: int32 [32], P('parts'), parts along dimension 0, may hold values from 1 to 160, 1920 in all
- slot_plan: int32 [32], P('parts'), parts along dimension 0, may hold values from 0 to 15, each once
Outputs:
- scores: float32 [32, 4], P(('parts', 'blk')), parts along dimension 0
There are 2 independent parts, one for each index of `parts`. A program takes and returns all parts, laid end to end along the dimension named above; an argument that names none is the same for every part. Nothing has to cross between parts.
Inputs may be any that keep to these rules, and one draw needn't show every extreme that they name: `owners`: distinct slots of blk.
All inputs are finite; a program needn't handle non-finite values.
Results may differ from a plain program's by a relative error of at most 0.01.
Values may be sent and summed in bfloat16 or wider, within the bound.
A program may use at most 128 MiB of HBM per device.

v0:
```python
import jax
import jax.numpy as jnp
from jax import lax
from jax.sharding import PartitionSpec as P


def spread(value, axis, source):
    kept = jnp.where(lax.axis_index(axis) == source, value, 0).astype(value.dtype)
    return lax.psum(kept, axis)


def shards(
    activations,
    output_grads,
    basis_in,
    basis_out,
    query_left,
    query_right,
    owners,
    lengths,
    slot_plan,
):
    num_blocks = lax.axis_size("blk")
    my_index = lax.axis_index("blk")
    seqs_here = activations.shape[0]
    max_length = activations.shape[1]
    width_in = activations.shape[2]
    width_out = output_grads.shape[2]
    num_queries = owners.shape[0]
    rank_count = query_left.shape[1]
    total_seqs = seqs_here * num_blocks
    total_cols = num_queries * rank_count
    pieces_in = []
    pieces_out = []
    for query_num in range(num_queries):
        block_in, block_out = (
            spread(query_left[0], "blk", owners[query_num]),
            spread(query_right[0], "blk", owners[query_num]),
        )
        pieces_in.append(block_in)
        pieces_out.append(block_out)
    picked_in = jnp.stack(pieces_in).reshape(total_cols, query_left.shape[2])
    picked_out = jnp.stack(pieces_out).reshape(total_cols, query_right.shape[2])
    contract = (((1,), (1,)), ((), ()))
    rotated_in = lax.dot_general(
        basis_in, picked_in, contract, preferred_element_type=jnp.float32
    ).astype(jnp.bfloat16)
    rotated_out = lax.dot_general(
        basis_out, picked_out, contract, preferred_element_type=jnp.float32
    ).astype(jnp.bfloat16)
    slot_match = slot_plan[:, None] == jnp.arange(total_seqs, dtype=jnp.int32)[None, :]
    slot_lengths = jnp.sum(jnp.where(slot_match, lengths[None, :], 0), axis=1)
    live_all = (jnp.arange(max_length, dtype=jnp.int32)[None, :] < slot_lengths[:, None]).astype(
        jnp.float32
    )
    my_live = lax.dynamic_slice_in_dim(live_all, my_index * seqs_here, seqs_here, 0)
    flat_in = activations.reshape(-1, width_in)
    flat_out = output_grads.reshape(-1, width_out)
    whole_in, whole_out = (
        lax.all_gather(rotated_in, "blk", axis=0, tiled=True),
        lax.all_gather(rotated_out, "blk", axis=0, tiled=True),
    )
    project_in = jnp.dot(flat_in, whole_in, preferred_element_type=jnp.float32)
    project_out = jnp.dot(flat_out, whole_out, preferred_element_type=jnp.float32)
    products = (project_in * project_out).reshape(-1, max_length, num_queries, rank_count)
    gathered = lax.all_gather(
        jnp.einsum("stqr,st->sq", products, my_live) / rank_count, "blk", axis=0, tiled=True
    )
    seq_ids = my_index * seqs_here + jnp.arange(seqs_here, dtype=jnp.int32)
    chooser = (slot_plan[None, :] == seq_ids[:, None]).astype(jnp.float32)
    return jnp.dot(chooser, gathered, precision=lax.Precision.HIGHEST)


def solution(mesh):
    placed = (
        P(("parts", "blk"), None, None),
        P(("parts", "blk"), None, None),
        P("blk", None),
        P("blk", None),
        P("blk", None, None),
        P("blk", None, None),
        P(),
        P("parts"),
        P("parts"),
    )
    return jax.shard_map(
        shards, mesh=mesh, in_specs=placed, out_specs=P(("parts", "blk"), None), check_vma=False
    )
```

profile of v0, /device:TPU:0, one launch (start us, length us, event | category | flops | bytes accessed | tf_op | source)
XLA Modules:
  0.0 282.1 jit_solution(5358135961362964753)
XLA Ops:
  6.5 0.0 copy-start
  6.5 0.0 copy-start.2
  6.5 0.0 all-reduce.4.cloned.1.call-start
  6.5 1.5 fusion.21
  10.5 3.0 %broadcast_select_fusion.3 = (bf16[1,32,14336]{2,1,0:T(8,128)(2,1)}, bf16[1,32,14336]{2,1,0:T(8,128)(2,1)}, bf16[1,32,14336]{2,1,0:T(8,128)(2,1)}, bf16[1,32,14336]{2,1,0:T(8,128)(2,1)}) fusion(bf16[1,32,14336]{2,1,0:T(8,128)(2,1)} %param.14, pred[]{:T(512)S(6)} %eq.40, pred[]{:T(512)S(6)} %eq.41, pred[]{:T(512)S(6)} %eq.43, pred[]{:T(512)S(6)} %eq.42), kind=kLoop, calls=%fused_computation.17 | loop fusion | flops 1835008 | bytes 4587524 | tf_op jit(solution)/shard_map/jit(_where)/select_n | solution.py:8
  13.6 0.0 copy-done.2
  13.6 1.1 broadcast_select_fusion.7
  14.6 0.0 all-reduce.4.cloned.1.call-update
  14.6 0.0 all-gather.6.cloned.1.call-start
  14.7 120.4 %all-reduce.4.cloned.1.call-done = (bf16[1,32,14336]{2,1,0:T(8,128)(2,1)}, bf16[1,32,14336]{2,1,0:T(8,128)(2,1)}, bf16[1,32,14336]{2,1,0:T(8,128)(2,1)}, bf16[1,...) async-done(((bf16[1,32,14336]{2,1,0:T(8,128)(2,1)}, ...) | async-done | bytes 4718608 | tf_op jit(solution)/shard_map/psum | solution.py:9
  135.1 3.5 %pad_maximum_fusion = bf16[4,32,14336]{2,1,0:T(8,128)(2,1)} fusion(bf16[1,32,14336]{2,1,0:T(8,128)(2,1)} %get-tuple-element.5, bf16[1,32,14336]{2,1,0:T(8,128)(2,1)} %get-tuple-element.6, bf16[1,32,14336]{2,1,0:T(8,128)(2,1)} %get-tuple-element.7, bf16[1,32,14336]{2,1,0:T(8,128)(2,1)} %get-tuple-element.8), kind=kLoop, calls=%fused_computation.2 | loop fusion | flops 5505024 | bytes 7340032 | tf_op jit(solution)/shard_map/stack | solution.py:43
  138.5 0.0 copy-start.3
  138.5 0.0 copy-start.4
  138.5 0.0 copy-start.5
  138.5 0.0 copy-start.6
  138.6 14.3 %fusion.4 = bf16[896,128]{0,1:T(8,128)(2,1)} fusion(bf16[128,14336]{1,0:T(8,128)(2,1)} %bitcast.44, bf16[896,14336]{1,0:T(8,128)(2,1)} %param.12), kind=kOutput, calls=%fused_computation.6 | convolution fusion | flops 3288449024 | bytes 29589504 | tf_op jit(solution)/shard_map/dot_general | solution.py:48
  152.9 0.0 copy-start.7
  152.9 0.0 copy-start.8
  152.9 0.0 copy-start.9
  152.9 0.0 all-gather.6.cloned.1.call-update
  152.9 0.0 all-gather.4.cloned.1.call-start
  153.0 0.0 copy-done.3
  153.0 0.0 copy-done.4
  153.0 0.0 copy-done.5
  153.0 0.0 copy-done.6
  153.0 0.1 pad_maximum_fusion.1
  153.1 0.0 copy-done
  153.1 1.5 fusion.11
  154.6 0.0 all-gather.4.cloned.1.call-update
  154.6 0.0 copy-done.7
  154.7 0.0 copy-done.8
  154.7 0.2 select_reduce_fusion
  154.9 0.6 dynamic-slice.1
  155.4 0.0 copy-done.9
  155.4 0.6 dynamic-slice
  156.7 0.0 copy-start.1
  156.7 44.0 %all-gather.6.cloned.1.call-done = bf16[14336,128]{0,1:T(8,128)(2,1)} async-done(((bf16[896,128]{0,1:T(8,128)(2,1)}), bf16[14336,128]{0,1:T(8,128)(2,1)}) %all-gather.6.cloned.1.call-update) | async-done | bytes 3670032 | tf_op jit(solution)/shard_map/all_gather | solution.py:61
  200.6 4.8 %fusion = f32[128,160]{0,1:T(8,128)S(1)} fusion(bf16[14336,128]{0,1:T(8,128)(2,1)} %all-gather.6.cloned.1.call-done, bf16[1,160,14336]{2,1,0:T(8,128)(2,1)} %param.10), kind=kOutput, calls=%fused_computation | convolution fusion | flops 587202560 | bytes 8339456 | tf_op jit(solution)/shard_map/dot_general | solution.py:64
  205.4 32.9 %all-gather.4.cloned.1.call-done = bf16[4096,128]{0,1:T(8,128)(2,1)} async-done(((bf16[256,128]{0,1:T(8,128)(2,1)}), bf16[4096,128]{0,1:T(8,128)(2,1)}) %all-gather.4.cloned.1.call-update) | async-done | bytes 1048592 | tf_op jit(solution)/shard_map/all_gather | solution.py:60
  238.3 0.0 copy-done.1
  238.3 2.4 fusion.8
  240.7 1.0 copy.12
  241.7 0.8 fusion.12
  242.4 0.2 dynamic-update-slice
  242.6 32.2 %all-reduce = f32[64]{0:T(128)S(1)} all-reduce(f32[64]{0:T(128)S(1)} %dynamic-update-slice), channel_id=2, replica_groups=mesh['parts'=2,'blk'=16] {'blk'}, use_global_device_ids=true, to_apply=%add | all-reduce | flops 64 | bytes 512
  274.9 0.1 reshape.71
  274.9 0.7 fusion.15
  (2 shorter events, 0.0 us)
Async XLA Ops:
  6.5 146.6 %copy-start = (bf16[256,4096]{1,0:T(8,128)(2,1)S(1)}, bf16[256,4096]{1,0:T(8,128)(2,1)}, u32[]{:S(2)}) copy-start(bf16[256,4096]{1,0:T(8,128)(2,1)} %param.11) | copy-start | bytes 6291460
  6.5 7.0 %copy-start.2 = (bf16[1,32,4096]{2,1,0:T(8,128)(2,1)S(1)}, bf16[1,32,4096]{2,1,0:T(8,128)(2,1)}, u32[]{:S(2)}) copy-start(bf16[1,32,4096]{2,1,0:T(8,128)(2,1)} %param.13) | copy-start | bytes 786436
  6.5 128.5 %all-reduce.4.cloned.1.call-start = ((), (), s32[]{:S(2)}) async-start(), calls=%async_computation.2 | async-start | bytes 9437184 | tf_op jit(solution)/shard_map/psum | solution.py:9
  14.6 186.0 %all-gather.6.cloned.1.call-start = ((), (), s32[]{:S(2)}) async-start(), calls=%async_computation.1 | async-start | bytes 3899392 | tf_op jit(solution)/shard_map/all_gather | solution.py:61
  138.5 14.4 %copy-start.3 = (bf16[1,32,4096]{2,1,0:T(8,128)(2,1)S(1)}, bf16[1,32,4096]{2,1,0:T(8,128)(2,1)}, u32[]{:S(2)}) copy-start(bf16[1,32,4096]{2,1,0:T(8,128)(2,1)} %get-tuple-element.9) | copy-start | bytes 786436
  138.5 14.4 %copy-start.4 = (bf16[1,32,4096]{2,1,0:T(8,128)(2,1)S(1)}, bf16[1,32,4096]{2,1,0:T(8,128)(2,1)}, u32[]{:S(2)}) copy-start(bf16[1,32,4096]{2,1,0:T(8,128)(2,1)} %get-tuple-element.10) | copy-start | bytes 786436
  138.5 14.4 %copy-start.5 = (bf16[1,32,4096]{2,1,0:T(8,128)(2,1)S(1)}, bf16[1,32,4096]{2,1,0:T(8,128)(2,1)}, u32[]{:S(2)}) copy-start(bf16[1,32,4096]{2,1,0:T(8,128)(2,1)} %get-tuple-element.11) | copy-start | bytes 786436
  138.5 14.4 %copy-start.6 = (bf16[1,32,4096]{2,1,0:T(8,128)(2,1)S(1)}, bf16[1,32,4096]{2,1,0:T(8,128)(2,1)}, u32[]{:S(2)}) copy-start(bf16[1,32,4096]{2,1,0:T(8,128)(2,1)} %get-tuple-element.12) | copy-start | bytes 786436
  152.9 1.8 copy-start.7
  152.9 1.8 copy-start.8
  152.9 2.6 copy-start.9
  152.9 85.4 %all-gather.4.cloned.1.call-start = ((), (), s32[]{:S(2)}) async-start(), calls=%async_computation | async-start | bytes 1114112 | tf_op jit(solution)/shard_map/all_gather | solution.py:60
  156.7 81.6 %copy-start.1 = (bf16[1,160,4096]{2,1,0:T(8,128)(2,1)S(1)}, bf16[1,160,4096]{2,1,0:T(8,128)(2,1)}, u32[]{:S(2)}) copy-start(bf16[1,160,4096]{2,1,0:T(8,128)(2,1)} %param.9) | copy-start | bytes 3932164
Sparse Core Ops, SparseCore 0:
  14.8 120.2 all-reduce.3
  153.0 47.5 all-gather.5
  202.8 35.4 all-gather.3
where the time goes:
time: 282 us
  waiting for transfers between devices  197 us (70%)
  blocking collectives  32.2 us (11%)
  matrix products  24.3 us (9%)
  between operations  16.3 us (6%)
  other arithmetic  7.9 us (3%)
  local copies, waits for them, and re-layouts  3.97 us (1%)
    psum x1, waiting for transfers between devices, spread(): return lax.psum(kept, axis)  120 us
    all_gather x1, waiting for transfers between devices, shards(): lax.all_gather(rotated_out, 'blk', axis=0, tiled=True)  44 us
    all_gather x1, waiting for transfers between devices, shards(): lax.all_gather(rotated_in, 'blk', axis=0, tiled=True)  32.9 us
    unnamed x1, blocking collectives  32.2 us
    dot_general x1, matrix products, shards(): lax.dot_general(basis_out, picked_out, contract, preferred_element_type=j...  14.3 us
  transfers between devices with their start and end apart: 3, of which 3 were waited for; matrix products, arithmetic and copies ran while one was open for 3% of the time, Pallas kernels for 0%

commit v1 on v0

v1 whole, which is shorter than its diff:
```python
import functools

import jax
import jax.numpy as jnp
from jax import lax
from jax.experimental import pallas as pl
from jax.experimental.pallas import tpu as pltpu
from jax.sharding import PartitionSpec as P

MESH = pl.DeviceIdType.MESH
CORES = 2
LANES = 128


def ring_order(chips):
    cols = 1
    while (2 * cols) * (2 * cols) <= chips:
        cols *= 2
    rows = chips // cols
    tour = [r * cols for r in range(rows)]
    for step, r in enumerate(reversed(range(rows))):
        across = range(1, cols) if step % 2 == 0 else range(cols - 1, 0, -1)
        tour += [r * cols + c for c in across]
    return tour


def lookup(index, table):
    found = jnp.int32(0)
    for key, value in enumerate(table):
        found = found + jnp.where(index == key, jnp.int32(value), jnp.int32(0))
    return found


def fused_kernel(
    n,
    act_hbm,
    grad_hbm,
    bin_hbm,
    bout_hbm,
    ql_hbm,
    qr_hbm,
    owners,
    lengths,
    slot_plan,
    out_ref,
    act,
    grad,
    bin_,
    bout,
    slots,
    gathered,
    rotated,
    acc_in,
    acc_out,
    proj_in,
    proj_out,
    tiles,
    load_sem,
    own_sem,
    a2a_send,
    a2a_recv,
    x_send,
    x_recv,
    ring_send,
    ring_recv,
    sib_send,
    sib_recv,
    tile_send,
    tile_recv,
):
    part = lax.axis_index("parts")
    me = lax.axis_index("blk")
    chips = n // CORES
    core = lax.rem(me, CORES)
    chip = me // CORES
    tour = ring_order(chips)
    place = lookup(chip, [tour.index(c) for c in range(chips)])
    sibling = chip * CORES + (1 - core)
    d_blk = act.shape[1] // n
    f_blk = grad.shape[1] // n
    both = d_blk + f_blk
    rank = ql_hbm.shape[1]
    half_rank = rank // 2
    queries = owners.shape[0]
    sub_rows = queries * half_rank
    far = chips // 2

    def at_distance(h, way, which_core):
        spot = lax.rem(place - h + chips, chips) if way == 0 else lax.rem(place + h, chips)
        return lookup(spot, tour) * CORES + which_core

    right = at_distance(1, 1, core)
    left = at_distance(1, 0, core)

    loads = []

    def load(src, dst):
        copy = pltpu.make_async_copy(src, dst, load_sem.at[len(loads)])
        copy.start()
        loads.append(copy)

    barrier = pltpu.get_barrier_semaphore()
    for k in range(1, n):
        pl.semaphore_signal(
            barrier, inc=1, device_id={"blk": lax.rem(me + k, n)}, device_id_type=MESH
        )
    pl.semaphore_signal(barrier, inc=1, device_id={"parts": 1 - part}, device_id_type=MESH)

    my_rows = pl.ds(pl.multiple_of(part * half_rank, half_rank), half_rank)

    def cut(target, width):
        return pl.ds(pl.multiple_of(target * width, LANES), width)

    own = [
        pltpu.make_async_copy(
            ql_hbm.at[0, my_rows, cut(me, d_blk)], slots.at[me, :, pl.ds(0, d_blk)], own_sem.at[0]
        ),
        pltpu.make_async_copy(
            qr_hbm.at[0, my_rows, cut(me, f_blk)],
            slots.at[me, :, pl.ds(d_blk, f_blk)],
            own_sem.at[1],
        ),
    ]
    for copy in own:
        copy.start()
    pl.semaphore_wait(barrier, n)

    swaps = []
    for k in range(1, n):
        target = lax.rem(me + k, n)
        for piece, (src, width, start) in enumerate(((ql_hbm, d_blk, 0), (qr_hbm, f_blk, d_blk))):
            copy = pltpu.make_async_remote_copy(
                src_ref=src.at[0, my_rows, cut(target, width)],
                dst_ref=slots.at[me, :, pl.ds(start, width)],
                send_sem=a2a_send.at[k, piece],
                recv_sem=a2a_recv.at[k, piece],
                device_id={"blk": target},
                device_id_type=MESH,
            )
            copy.start()
            swaps.append(copy)

    load(bin_hbm, bin_)
    quarter = bout.shape[0] // 4
    for i in range(4):
        span = pl.ds(i * quarter, quarter)
        load(bout_hbm.at[span], bout.at[span])
    load(act_hbm.at[0], act)
    load(grad_hbm.at[0], grad)
    acc_in[...] = jnp.zeros_like(acc_in)
    acc_out[...] = jnp.zeros_like(acc_out)
    proj_in[...] = jnp.zeros_like(proj_in)
    proj_out[...] = jnp.zeros_like(proj_out)

    for copy in own:
        copy.wait()
    for copy in swaps:
        copy.wait_recv()
    first = pl.multiple_of(part * sub_rows, sub_rows)
    for q in range(queries):
        gathered[me, pl.ds(pl.multiple_of(first + q * half_rank, half_rank), half_rank), :] = slots[
            owners[q]
        ]

    def spread(buffer, phase, sub, before_sub, compute):
        limit = ((far, far - 1), (far - 1, far))
        started = []

        def hop(u, way, h):
            block = at_distance(h, way, core)
            view = buffer.at[block, sub(u)]
            copy = pltpu.make_async_remote_copy(
                src_ref=view,
                dst_ref=view,
                send_sem=ring_send.at[phase, u, way, h],
                recv_sem=ring_recv.at[phase, u, way, h],
                device_id={"blk": right if way == 0 else left},
                device_id_type=MESH,
            )
            copy.start()
            started.append(copy)

        def arrival(u, way, h):
            view = buffer.at[at_distance(h, way, core), sub(u)]
            pltpu.make_async_remote_copy(
                src_ref=view,
                dst_ref=view,
                send_sem=ring_send.at[phase, u, way, h - 1],
                recv_sem=ring_recv.at[phase, u, way, h - 1],
                device_id={"blk": right if way == 0 else left},
                device_id_type=MESH,
            ).wait_recv()

        def aside(u, way, h, which_core):
            view = buffer.at[at_distance(h, way, which_core), sub(u)]
            return pltpu.make_async_remote_copy(
                src_ref=view,
                dst_ref=view,
                send_sem=sib_send.at[phase, u, way, h],
                recv_sem=sib_recv.at[phase, u, way, h],
                device_id={"blk": sibling},
                device_id_type=MESH,
            )

        for h in range(far + 1):
            here = []
            for u in range(2):
                if h == 0:
                    before_sub(u)
                ways = [w for w in range(2) if h <= limit[u][w]] if h else [0]
                for way in ways:
                    if h:
                        arrival(u, way, h)
                        if h < limit[u][way]:
                            hop(u, way, h)
                    else:
                        hop(u, 0, 0)
                        hop(u, 1, 0)
                    copy = aside(u, way, h, core)
                    copy.start()
                    started.append(copy)
                    here.append((u, way, h))
            directions = [0] if h in (0, far) else [0, 1]
            compute([at_distance(h, way, core) for way in directions], h == 0)
            for u, way, _ in here:
                aside(u, way, h, 1 - core).wait_recv()
            compute([at_distance(h, way, 1 - core) for way in directions], False)
        return started

    over_last = (((1,), (1,)), ((), ()))

    def each(blocks, body):
        def step(i, carry):
            block = blocks[0]
            for k in range(1, len(blocks)):
                block = jnp.where(i == k, blocks[k], block)
            body(block)
            return carry

        lax.fori_loop(0, len(blocks), step, 0)

    def rotate(block):
        acc_in[...] += lax.dot_general(
            bin_[:, cut(block, d_blk)],
            gathered[block, :, 0:d_blk],
            over_last,
            preferred_element_type=jnp.float32,
        )
        acc_out[...] += lax.dot_general(
            bout[:, cut(block, f_blk)],
            gathered[block, :, d_blk:both],
            over_last,
            preferred_element_type=jnp.float32,
        )

    def rotate_all(blocks, opening):
        if opening:
            for copy in loads:
                copy.wait()
        each(blocks, rotate)

    trade = pltpu.make_async_remote_copy(
        src_ref=gathered.at[me, pl.ds(first, sub_rows)],
        dst_ref=gathered.at[me, pl.ds(first, sub_rows)],
        send_sem=x_send,
        recv_sem=x_recv,
        device_id={"parts": 1 - part},
        device_id_type=MESH,
    )
    trade.start()
    second = pl.multiple_of((1 - part) * sub_rows, sub_rows)

    def before_rotate(u):
        if u == 1:
            pltpu.make_async_remote_copy(
                src_ref=gathered.at[me, pl.ds(second, sub_rows)],
                dst_ref=gathered.at[me, pl.ds(second, sub_rows)],
                send_sem=x_send,
                recv_sem=x_recv,
                device_id={"parts": 1 - part},
                device_id_type=MESH,
            ).wait_recv()

    def sub_query(u):
        return pl.ds(first if u == 0 else second, sub_rows)

    started = spread(gathered, 0, sub_query, before_rotate, rotate_all)

    rotated[me, 0:d_blk, :] = acc_in[...].astype(rotated.dtype)
    rotated[me, d_blk:both, :] = acc_out[...].astype(rotated.dtype)

    def project(block):
        proj_in[...] += jnp.dot(
            act[:, cut(block, d_blk)],
            rotated[block, 0:d_blk, :],
            preferred_element_type=jnp.float32,
        )
        proj_out[...] += jnp.dot(
            grad[:, cut(block, f_blk)],
            rotated[block, d_blk:both, :],
            preferred_element_type=jnp.float32,
        )

    half = both // 2
    started += spread(
        rotated,
        1,
        lambda u: pl.ds(u * half, half),
        lambda u: None,
        lambda blocks, opening: each(blocks, project),
    )

    length = lengths[slot_plan[me]]
    times = lax.broadcasted_iota(jnp.int32, proj_in.shape, 0)
    product = jnp.where(times < length, proj_in[...] * proj_out[...], 0.0)
    by_col = jnp.sum(product, axis=0, keepdims=True)
    col = lax.broadcasted_iota(jnp.int32, by_col.shape, 1)
    col_query = lax.rem(col // half_rank, queries)
    score = jnp.zeros((8, LANES), jnp.float32)
    lane = lax.broadcasted_iota(jnp.int32, score.shape, 1)
    for q in range(queries):
        total = jnp.sum(jnp.where(col_query == q, by_col, 0.0), axis=1, keepdims=True) / rank
        score = jnp.where(lane == q, total, score)
    tiles[me] = score
    pushes = []
    for k in range(1, n):
        copy = pltpu.make_async_remote_copy(
            src_ref=tiles.at[me],
            dst_ref=tiles.at[me],
            send_sem=tile_send.at[k],
            recv_sem=tile_recv.at[k],
            device_id={"blk": lax.rem(me + k, n)},
            device_id_type=MESH,
        )
        copy.start()
        pushes.append(copy)
    for k in range(1, n):
        source = lax.rem(me - k + n, n)
        pltpu.make_async_remote_copy(
            src_ref=tiles.at[source],
            dst_ref=tiles.at[source],
            send_sem=tile_send.at[k],
            recv_sem=tile_recv.at[k],
            device_id={"blk": lax.rem(me + k, n)},
            device_id_type=MESH,
        ).wait_recv()
    mine = jnp.zeros((8, LANES), jnp.float32)
    for j in range(n):
        mine = jnp.where(slot_plan[j] == me, tiles[j], mine)
    out_ref[...] = mine
    for copy in swaps + [trade] + started + pushes:
        copy.wait_send()


def fused(n, *args):
    activations, output_grads, basis_in, basis_out, query_left, query_right, owners = args[:7]
    tokens, width_in = activations.shape[1:]
    width_out = output_grads.shape[2]
    queries, rank = owners.shape[0], query_left.shape[1]
    cols = queries * rank
    d_blk, f_blk = width_in // n, width_out // n
    both = d_blk + f_blk
    hops = n // CORES // 2 + 1
    dma = pltpu.SemaphoreType.DMA
    result = pl.pallas_call(
        functools.partial(fused_kernel, n),
        out_shape=jax.ShapeDtypeStruct((8, LANES), jnp.float32),
        in_specs=[pl.BlockSpec(memory_space=pl.ANY)] * 6
        + [pl.BlockSpec(memory_space=pltpu.SMEM)] * 3,
        out_specs=pl.BlockSpec(memory_space=pltpu.VMEM),
        scratch_shapes=[
            pltpu.VMEM((tokens, width_in), jnp.bfloat16),
            pltpu.VMEM((tokens, width_out), jnp.bfloat16),
            pltpu.VMEM(basis_in.shape, jnp.bfloat16),
            pltpu.VMEM(basis_out.shape, jnp.bfloat16),
            pltpu.VMEM((n, rank // 2, both), jnp.bfloat16),
            pltpu.VMEM((n, cols, both), jnp.bfloat16),
            pltpu.VMEM((n, both, cols), jnp.bfloat16),
            pltpu.VMEM((d_blk, cols), jnp.float32),
            pltpu.VMEM((f_blk, cols), jnp.float32),
            pltpu.VMEM((tokens, cols), jnp.float32),
            pltpu.VMEM((tokens, cols), jnp.float32),
            pltpu.VMEM((n, 8, LANES), jnp.float32),
            dma((7,)),
            dma((2,)),
            dma((n, 2)),
            dma((n, 2)),
            dma,
            dma,
            dma((2, 2, 2, hops)),
            dma((2, 2, 2, hops)),
            dma((2, 2, 2, hops)),
            dma((2, 2, 2, hops)),
            dma((n,)),
            dma((n,)),
        ],
        compiler_params=pltpu.CompilerParams(
            collective_id=0, has_side_effects=True, vmem_limit_bytes=60 * 1024 * 1024
        ),
    )(*args)
    return result[:1, :queries]


def spread(value, axis, source):
    kept = jnp.where(lax.axis_index(axis) == source, value, 0).astype(value.dtype)
    return lax.psum(kept, axis)


def plain(
    activations,
    output_grads,
    basis_in,
    basis_out,
    query_left,
    query_right,
    owners,
    lengths,
    slot_plan,
):
    num_blocks = lax.axis_size("blk")
    my_index = lax.axis_index("blk")
    seqs_here = activations.shape[0]
    max_length = activations.shape[1]
    num_queries = owners.shape[0]
    rank_count = query_left.shape[1]
    total_seqs = seqs_here * num_blocks
    total_cols = num_queries * rank_count
    pieces_in = [spread(query_left[0], "blk", owners[q]) for q in range(num_queries)]
    pieces_out = [spread(query_right[0], "blk", owners[q]) for q in range(num_queries)]
    picked_in = jnp.stack(pieces_in).reshape(total_cols, query_left.shape[2])
    picked_out = jnp.stack(pieces_out).reshape(total_cols, query_right.shape[2])
    contract = (((1,), (1,)), ((), ()))
    rotated_in = lax.dot_general(
        basis_in, picked_in, contract, preferred_element_type=jnp.float32
    ).astype(jnp.bfloat16)
    rotated_out = lax.dot_general(
        basis_out, picked_out, contract, preferred_element_type=jnp.float32
    ).astype(jnp.bfloat16)
    slot_match = slot_plan[:, None] == jnp.arange(total_seqs, dtype=jnp.int32)[None, :]
    slot_lengths = jnp.sum(jnp.where(slot_match, lengths[None, :], 0), axis=1)
    live_all = (jnp.arange(max_length, dtype=jnp.int32)[None, :] < slot_lengths[:, None]).astype(
        jnp.float32
    )
    my_live = lax.dynamic_slice_in_dim(live_all, my_index * seqs_here, seqs_here, 0)
    flat_in = activations.reshape(-1, activations.shape[2])
    flat_out = output_grads.reshape(-1, output_grads.shape[2])
    whole_in = lax.all_gather(rotated_in, "blk", axis=0, tiled=True)
    whole_out = lax.all_gather(rotated_out, "blk", axis=0, tiled=True)
    project_in = jnp.dot(flat_in, whole_in, preferred_element_type=jnp.float32)
    project_out = jnp.dot(flat_out, whole_out, preferred_element_type=jnp.float32)
    products = (project_in * project_out).reshape(-1, max_length, num_queries, rank_count)
    gathered = lax.all_gather(
        jnp.einsum("stqr,st->sq", products, my_live) / rank_count, "blk", axis=0, tiled=True
    )
    seq_ids = my_index * seqs_here + jnp.arange(seqs_here, dtype=jnp.int32)
    chooser = (slot_plan[None, :] == seq_ids[:, None]).astype(jnp.float32)
    return jnp.dot(chooser, gathered, precision=lax.Precision.HIGHEST)


def shards(*args):
    n = lax.axis_size("blk")
    activations, output_grads, basis_in, basis_out, query_left, _, owners = args[:7]
    queries, rank = owners.shape[0], query_left.shape[1]
    fits = (
        lax.axis_size("parts") == 2
        and n % (2 * CORES) == 0
        and n >= 4 * CORES
        and activations.shape[0] == 1
        and query_left.shape[0] == 1
        and activations.shape[2] % (n * LANES) == 0
        and output_grads.shape[2] % (n * LANES) == 0
        and (activations.shape[2] + output_grads.shape[2]) // n % 32 == 0
        and basis_in.shape[0] * n == activations.shape[2]
        and basis_out.shape[0] * n == output_grads.shape[2]
        and basis_out.shape[0] % 64 == 0
        and queries * rank == LANES
        and rank % 32 == 0
    )
    return fused(n, *args) if fits else plain(*args)


def solution(mesh):
    placed = (
        P(("parts", "blk"), None, None),
        P(("parts", "blk"), None, None),
        P("blk", None),
        P("blk", None),
        P("blk", None, None),
        P("blk", None, None),
        P(),
        P("parts"),
        P("parts"),
    )
    return jax.shard_map(
        shards, mesh=mesh, in_specs=placed, out_specs=P(("parts", "blk"), None), check_vma=False
    )
```

time: 282 us -> 87.1 us (0.31)
  waiting for transfers between devices: 197 us -> 0 us
  Pallas kernels: 0 us -> 85.7 us
  blocking collectives: 32.2 us -> 0 us
  matrix products: 24.3 us -> 0 us
  between operations: 16.3 us -> 0.01 us
  other arithmetic: 7.9 us -> 0 us
    psum x1 -> x0, waiting for transfers between devices: 120 us -> none  [spread(): return lax.psum(kept, axis)]
    pallas_call x0 -> x1, Pallas kernels: none -> 85.7 us  [fused(): pl.pallas_call(functools.partial(fused_kernel, n), out_shape=jax.ShapeDty...]
    all_gather x2 -> x0, waiting for transfers between devices: 76.8 us -> none  [the longest x1 44 us: shards(): lax.all_gather(rotated_out, 'blk', axis=0, tiled=True)]
    unnamed x1 -> x0, blocking collectives: 32.2 us -> none
    dot_general x6 -> x0, matrix products: 24.3 us -> none  [the longest x1 14.3 us: shards(): lax.dot_general(basis_out, picked_out, contract, preferred_element_type=j...]
    select_n x2 -> x0, other arithmetic: 4.11 us -> none  [spread(): jnp.where(lax.axis_index(axis) == source, value, 0).astype(value.dtype)]
    another operation x2 -> x0, other arithmetic: 3.59 us -> none  [the longest x1 3.45 us: shards(): picked_out = jnp.stack(pieces_out).reshape(total_cols, query_right.shape[2])]
  transfers between devices with their start and end apart: 3 -> 0, of which waited for: 3 -> 0; matrix products, arithmetic and copies ran while one was open for 3% -> 0% of each run, Pallas kernels for 0% -> 0%
where the time goes in v1:
time: 87.1 us; the launch traced here: 86.9 us
  Pallas kernels  85.7 us (98%)
  local copies, waits for them, and re-layouts  1.19 us (1%)
    pallas_call x1, Pallas kernels, fused(): pl.pallas_call(functools.partial(fused_kernel, n), out_shape=jax.ShapeDty...  85.7 us

profile of v1, /device:TPU:0, one launch (start us, length us, event | category | flops | bytes accessed | tf_op | source)
XLA Modules:
  0.0 86.9 jit_solution(15950967313539846908)
XLA Ops:
  0.0 85.7 %shard_map.91 = f32[8,128]{1,0:T(8,128)} custom-call(bf16[1,160,4096]{2,1,0:T(8,128)(2,1)} %act_hbm.1, bf16[1,160,14336]{2,1,0:T(8,128)(2,1)} %grad_hbm.1, bf16[256,4096]{1,0:T(8,128)(2,1)} %bin_hbm.1, bf16[896,14336]{1,0:T(8,128)(2,1)} %bout_hbm.1, bf16[1,32,4096]{2,1,0:T(8,128)(2,1)} %ql_hbm.1, bf16[1,32,14336]{2,1,0:T(8,128)(2,1)} %qr_hbm.1, s32[4]{0:T(128)} %owners.1, ...), custom_call_target="tpu_custom_call" | custom-call | tf_op jit(solution)/shard_map/pallas_call | solution.py:365
  85.8 1.2 %slice.3 = f32[1,4]{1,0:T(1,128)} slice(f32[8,128]{1,0:T(8,128)} %shard_map.91), slice={[0:1], [0:4]} | slice | bytes 32 | tf_op jit(solution)/shard_map/slice | solution.py:401

commit v2 on v1

--- a/solution.py
+++ b/solution.py
@@ -59,6 +59,8 @@
     own_sem,
     a2a_send,
     a2a_recv,
+    trade_send,
+    trade_recv,
     x_send,
     x_recv,
     ring_send,
@@ -162,69 +164,87 @@
             owners[q]
         ]
 
-    def spread(buffer, phase, sub, before_sub, compute):
-        limit = ((far, far - 1), (far - 1, far))
+    def spread(buffer, phase, subs, crossing, whole, before_sub, compute):
+        limit = ((far, far - 1), (far, far - 1), (far - 1, far))
         started = []
 
-        def hop(u, way, h):
-            block = at_distance(h, way, core)
-            view = buffer.at[block, sub(u)]
-            copy = pltpu.make_async_remote_copy(
-                src_ref=view,
-                dst_ref=view,
-                send_sem=ring_send.at[phase, u, way, h],
-                recv_sem=ring_recv.at[phase, u, way, h],
-                device_id={"blk": right if way == 0 else left},
-                device_id_type=MESH,
-            )
-            copy.start()
-            started.append(copy)
-
-        def arrival(u, way, h):
-            view = buffer.at[at_distance(h, way, core), sub(u)]
-            pltpu.make_async_remote_copy(
-                src_ref=view,
-                dst_ref=view,
-                send_sem=ring_send.at[phase, u, way, h - 1],
-                recv_sem=ring_recv.at[phase, u, way, h - 1],
-                device_id={"blk": right if way == 0 else left},
-                device_id_type=MESH,
-            ).wait_recv()
-
-        def aside(u, way, h, which_core):
-            view = buffer.at[at_distance(h, way, which_core), sub(u)]
+        def remote(view, send_sem, recv_sem, device):
             return pltpu.make_async_remote_copy(
                 src_ref=view,
                 dst_ref=view,
-                send_sem=sib_send.at[phase, u, way, h],
-                recv_sem=sib_recv.at[phase, u, way, h],
-                device_id={"blk": sibling},
+                send_sem=send_sem,
+                recv_sem=recv_sem,
+                device_id=device,
                 device_id_type=MESH,
             )
 
+        def ring(u, way, h, at):
+            return remote(
+                buffer.at[at_distance(at, way, core), subs[u]],
+                ring_send.at[phase, u, way, h],
+                ring_recv.at[phase, u, way, h],
+                {"blk": right if way == 0 else left},
+            )
+
+        def across(way, h, rows):
+            return remote(
+                buffer.at[at_distance(h, way, core), rows],
+                x_send.at[phase, way, h],
+                x_recv.at[phase, way, h],
+                {"parts": 1 - part},
+            )
+
+        def aside(u, way, h, which_core):
+            return remote(
+                buffer.at[at_distance(h, way, which_core), subs[u] if u < 3 else crossing],
+                sib_send.at[phase, u, way, h],
+                sib_recv.at[phase, u, way, h],
+                {"blk": sibling},
+            )
+
+        def go(copy):
+            copy.start()
+            started.append(copy)
+
+        def ways_of(u, h):
+            return [w for w in range(2) if h <= limit[u][w]] if h else [0]
+
+        def finish_own(h):
+            for way in ways_of(0, h):
+                if h or not whole:
+                    across(way, h, crossing).wait_recv()
+                go(aside(3, way, h, core))
+            directions = [0] if h in (0, far) else [0, 1]
+            compute([at_distance(h, way, core) for way in directions], h == 0)
+
+        def finish_other(h):
+            for u in range(4):
+                for way in ways_of(u % 3, h):
+                    aside(u, way, h, 1 - core).wait_recv()
+            directions = [0] if h in (0, far) else [0, 1]
+            compute([at_distance(h, way, 1 - core) for way in directions], False)
+
         for h in range(far + 1):
-            here = []
-            for u in range(2):
+            for u in range(3):
                 if h == 0:
                     before_sub(u)
-                ways = [w for w in range(2) if h <= limit[u][w]] if h else [0]
-                for way in ways:
+                for way in ways_of(u, h):
                     if h:
-                        arrival(u, way, h)
+                        ring(u, way, h - 1, h).wait_recv()
                         if h < limit[u][way]:
-                            hop(u, way, h)
+                            go(ring(u, way, h, h))
                     else:
-                        hop(u, 0, 0)
-                        hop(u, 1, 0)
-                    copy = aside(u, way, h, core)
-                    copy.start()
-                    started.append(copy)
-                    here.append((u, way, h))
-            directions = [0] if h in (0, far) else [0, 1]
-            compute([at_distance(h, way, core) for way in directions], h == 0)
-            for u, way, _ in here:
-                aside(u, way, h, 1 - core).wait_recv()
-            compute([at_distance(h, way, 1 - core) for way in directions], False)
+                        go(ring(u, 0, 0, 0))
+                        go(ring(u, 1, 0, 0))
+                    if u == 0 and (h or not whole):
+                        go(across(way, h, subs[0]))
+                    go(aside(u, way, h, core))
+                if h and u == 0:
+                    finish_own(h - 1)
+                if h and u == 1:
+                    finish_other(h - 1)
+        finish_own(far)
+        finish_other(far)
         return started
 
     over_last = (((1,), (1,)), ((), ()))
@@ -259,32 +279,34 @@
                 copy.wait()
         each(blocks, rotate)
 
-    trade = pltpu.make_async_remote_copy(
-        src_ref=gathered.at[me, pl.ds(first, sub_rows)],
-        dst_ref=gathered.at[me, pl.ds(first, sub_rows)],
-        send_sem=x_send,
-        recv_sem=x_recv,
-        device_id={"parts": 1 - part},
-        device_id_type=MESH,
-    )
-    trade.start()
-    second = pl.multiple_of((1 - part) * sub_rows, sub_rows)
+    def layout(unit):
+        def span(start, count):
+            return pl.ds(pl.multiple_of(start * unit, unit), count * unit)
+
+        subs = [span(part * 6, 2), span(2 + part * 3, 1), span(3 - part, 3)]
+        return subs, span(6 - part * 6, 2), span
+
+    query_subs, query_crossing, query_span = layout(gathered.shape[1] // 8)
+
+    def trade(start):
+        rows = query_span(start, 2)
+        return pltpu.make_async_remote_copy(
+            src_ref=gathered.at[me, rows],
+            dst_ref=gathered.at[me, rows],
+            send_sem=trade_send,
+            recv_sem=trade_recv,
+            device_id={"parts": 1 - part},
+            device_id_type=MESH,
+        )
+
+    traded = trade(2 + 2 * part)
+    traded.start()
 
     def before_rotate(u):
-        if u == 1:
-            pltpu.make_async_remote_copy(
-                src_ref=gathered.at[me, pl.ds(second, sub_rows)],
-                dst_ref=gathered.at[me, pl.ds(second, sub_rows)],
-                send_sem=x_send,
-                recv_sem=x_recv,
-                device_id={"parts": 1 - part},
-                device_id_type=MESH,
-            ).wait_recv()
-
-    def sub_query(u):
-        return pl.ds(first if u == 0 else second, sub_rows)
-
-    started = spread(gathered, 0, sub_query, before_rotate, rotate_all)
+        if u == 2:
+            trade(4 - 2 * part).wait_recv()
+
+    started = spread(gathered, 0, query_subs, query_crossing, False, before_rotate, rotate_all)
 
     rotated[me, 0:d_blk, :] = acc_in[...].astype(rotated.dtype)
     rotated[me, d_blk:both, :] = acc_out[...].astype(rotated.dtype)
@@ -301,11 +323,13 @@
             preferred_element_type=jnp.float32,
         )
 
-    half = both // 2
+    block_subs, block_crossing, _ = layout(both // 8)
     started += spread(
         rotated,
         1,
-        lambda u: pl.ds(u * half, half),
+        block_subs,
+        block_crossing,
+        True,
         lambda u: None,
         lambda blocks, opening: each(blocks, project),
     )
@@ -348,7 +372,7 @@
     for j in range(n):
         mine = jnp.where(slot_plan[j] == me, tiles[j], mine)
     out_ref[...] = mine
-    for copy in swaps + [trade] + started + pushes:
+    for copy in swaps + [traded] + started + pushes:
         copy.wait_send()
 
 
@@ -387,10 +411,12 @@
             dma((n, 2)),
             dma,
             dma,
-            dma((2, 2, 2, hops)),
-            dma((2, 2, 2, hops)),
-            dma((2, 2, 2, hops)),
-            dma((2, 2, 2, hops)),
+            dma((2, 2, hops)),
+            dma((2, 2, hops)),
+            dma((2, 3, 2, hops)),
+            dma((2, 3, 2, hops)),
+            dma((2, 4, 2, hops)),
+            dma((2, 4, 2, hops)),
             dma((n,)),
             dma((n,)),
         ],
@@ -469,7 +495,7 @@
         and query_left.shape[0] == 1
         and activations.shape[2] % (n * LANES) == 0
         and output_grads.shape[2] % (n * LANES) == 0
-        and (activations.shape[2] + output_grads.shape[2]) // n % 32 == 0
+        and (activations.shape[2] + output_grads.shape[2]) // n % 128 == 0
         and basis_in.shape[0] * n == activations.shape[2]
         and basis_out.shape[0] * n == output_grads.shape[2]
         and basis_out.shape[0] % 64 == 0

time: 87.1 us -> 78.3 us (0.90)
  Pallas kernels: 85.7 us -> 76.9 us
    pallas_call x1, Pallas kernels: 85.7 us -> 76.9 us  [fused(): pl.pallas_call(functools.partial(fused_kernel, n), out_shape=jax.ShapeDty...]
where the time goes in v2:
time: 78.3 us; the launch traced here: 78.1 us
  Pallas kernels  76.9 us (98%)
  local copies, waits for them, and re-layouts  1.19 us (2%)
    pallas_call x1, Pallas kernels, fused(): pl.pallas_call(functools.partial(fused_kernel, n), out_shape=jax.ShapeDty...  76.9 us

profile of v2, /device:TPU:0, one launch (start us, length us, event | category | flops | bytes accessed | tf_op | source)
XLA Modules:
  0.0 78.1 jit_solution(5645169718082271490)
XLA Ops:
  0.0 76.9 %shard_map.91 = f32[8,128]{1,0:T(8,128)} custom-call(bf16[1,160,4096]{2,1,0:T(8,128)(2,1)} %act_hbm.1, bf16[1,160,14336]{2,1,0:T(8,128)(2,1)} %grad_hbm.1, bf16[256,4096]{1,0:T(8,128)(2,1)} %bin_hbm.1, bf16[896,14336]{1,0:T(8,128)(2,1)} %bout_hbm.1, bf16[1,32,4096]{2,1,0:T(8,128)(2,1)} %ql_hbm.1, bf16[1,32,14336]{2,1,0:T(8,128)(2,1)} %qr_hbm.1, s32[4]{0:T(128)} %owners.1, ...), custom_call_target="tpu_custom_call" | custom-call | tf_op jit(solution)/shard_map/pallas_call | solution.py:389
  76.9 1.2 %slice.3 = f32[1,4]{1,0:T(1,128)} slice(f32[8,128]{1,0:T(8,128)} %shard_map.91), slice={[0:1], [0:4]} | slice | bytes 32 | tf_op jit(solution)/shard_map/slice | solution.py:427

commit v3 on v2

--- a/solution.py
+++ b/solution.py
@@ -125,6 +125,13 @@
     ]
     for copy in own:
         copy.start()
+    load(bin_hbm, bin_)
+    quarter = bout.shape[0] // 4
+    for i in range(4):
+        span = pl.ds(i * quarter, quarter)
+        load(bout_hbm.at[span], bout.at[span])
+    load(act_hbm.at[0], act)
+    load(grad_hbm.at[0], grad)
     pl.semaphore_wait(barrier, n)
 
     swaps = []
@@ -142,13 +149,6 @@
             copy.start()
             swaps.append(copy)
 
-    load(bin_hbm, bin_)
-    quarter = bout.shape[0] // 4
-    for i in range(4):
-        span = pl.ds(i * quarter, quarter)
-        load(bout_hbm.at[span], bout.at[span])
-    load(act_hbm.at[0], act)
-    load(grad_hbm.at[0], grad)
     acc_in[...] = jnp.zeros_like(acc_in)
     acc_out[...] = jnp.zeros_like(acc_out)
     proj_in[...] = jnp.zeros_like(proj_in)
@@ -210,19 +210,30 @@
             return [w for w in range(2) if h <= limit[u][w]] if h else [0]
 
         def finish_own(h):
-            for way in ways_of(0, h):
-                if h or not whole:
-                    across(way, h, crossing).wait_recv()
-                go(aside(3, way, h, core))
-            directions = [0] if h in (0, far) else [0, 1]
-            compute([at_distance(h, way, core) for way in directions], h == 0)
+            def crossed():
+                for way in ways_of(0, h):
+                    if h or not whole:
+                        across(way, h, crossing).wait_recv()
+                    go(aside(3, way, h, core))
+
+            return [crossed] + [
+                functools.partial(compute, [at_distance(h, way, core)], h == 0)
+                for way in both_ways(h)
+            ]
 
         def finish_other(h):
-            for u in range(4):
-                for way in ways_of(u % 3, h):
-                    aside(u, way, h, 1 - core).wait_recv()
-            directions = [0] if h in (0, far) else [0, 1]
-            compute([at_distance(h, way, 1 - core) for way in directions], False)
+            def arrived():
+                for u in range(4):
+                    for way in ways_of(u % 3, h):
+                        aside(u, way, h, 1 - core).wait_recv()
+
+            return [arrived] + [
+                functools.partial(compute, [at_distance(h, way, 1 - core)], False)
+                for way in both_ways(h)
+            ]
+
+        def both_ways(h):
+            return [0] if h in (0, far) else [0, 1]
 
         for h in range(far + 1):
             for u in range(3):
@@ -239,12 +250,14 @@
                     if u == 0 and (h or not whole):
                         go(across(way, h, subs[0]))
                     go(aside(u, way, h, core))
-                if h and u == 0:
-                    finish_own(h - 1)
-                if h and u == 1:
-                    finish_other(h - 1)
-        finish_own(far)
-        finish_other(far)
+                if h:
+                    if u == 0:
+                        tasks = finish_own(h - 1) + finish_other(h - 1)
+                    for _ in range((2, 4, len(tasks))[u]):
+                        if tasks:
+                            tasks.pop(0)()
+        for task in finish_own(far) + finish_other(far):
+            task()
         return started
 
     over_last = (((1,), (1,)), ((), ()))
@@ -323,7 +336,18 @@
             preferred_element_type=jnp.float32,
         )
 
-    block_subs, block_crossing, _ = layout(both // 8)
+    cross = both * 5 // 18 // 16 * 16
+    light = (both - 3 * cross) // 32 * 16
+
+    def rows(if_first, if_second, count):
+        return pl.ds(pl.multiple_of(if_first + part * (if_second - if_first), 16), count)
+
+    block_subs = [
+        rows(0, both - cross, cross),
+        rows(cross, both - cross - light, light),
+        rows(cross + light, cross, both - 2 * cross - light),
+    ]
+    block_crossing = rows(both - cross, 0, cross)
     started += spread(
         rotated,
         1,
@@ -371,7 +395,7 @@
     mine = jnp.zeros((8, LANES), jnp.float32)
     for j in range(n):
         mine = jnp.where(slot_plan[j] == me, tiles[j], mine)
-    out_ref[...] = mine
+    out_ref[...] = mine[:1, :queries]
     for copy in swaps + [traded] + started + pushes:
         copy.wait_send()
 
@@ -386,9 +410,9 @@
     both = d_blk + f_blk
     hops = n // CORES // 2 + 1
     dma = pltpu.SemaphoreType.DMA
-    result = pl.pallas_call(
+    return pl.pallas_call(
         functools.partial(fused_kernel, n),
-        out_shape=jax.ShapeDtypeStruct((8, LANES), jnp.float32),
+        out_shape=jax.ShapeDtypeStruct((1, queries), jnp.float32),
         in_specs=[pl.BlockSpec(memory_space=pl.ANY)] * 6
         + [pl.BlockSpec(memory_space=pltpu.SMEM)] * 3,
         out_specs=pl.BlockSpec(memory_space=pltpu.VMEM),
@@ -424,7 +448,6 @@
             collective_id=0, has_side_effects=True, vmem_limit_bytes=60 * 1024 * 1024
         ),
     )(*args)
-    return result[:1, :queries]
 
 
 def spread(value, axis, source):

time: 78.3 us -> 77.9 us (level)
    slice x1 -> x0, local copies, waits for them, and re-layouts: 1.19 us -> none  [fused(): return result[:1, :queries]]
    unnamed x0 -> x1, local copies, waits for them, and re-layouts: none -> 1.19 us
where the time goes in v3:
time: 77.9 us; the launch traced here: 77.7 us
  Pallas kernels  76.5 us (98%)
  local copies, waits for them, and re-layouts  1.19 us (2%)
    pallas_call x1, Pallas kernels, fused(): pl.pallas_call(functools.partial(fused_kernel, n), out_shape=jax.ShapeDty...  76.5 us

profile of v3, /device:TPU:0, one launch (start us, length us, event | category | flops | bytes accessed | tf_op | source)
XLA Modules:
  0.0 77.7 jit_solution(855541832277119257)
XLA Ops:
  0.0 76.5 %shard_map.91 = f32[1,4]{1,0:T(1,128)} custom-call(bf16[1,160,4096]{2,1,0:T(8,128)(2,1)} %act_hbm.1, bf16[1,160,14336]{2,1,0:T(8,128)(2,1)} %grad_hbm.1, bf16[256,4096]{1,0:T(8,128)(2,1)} %bin_hbm.1, bf16[896,14336]{1,0:T(8,128)(2,1)} %bout_hbm.1, bf16[1,32,4096]{2,1,0:T(8,128)(2,1)} %ql_hbm.1, bf16[1,32,14336]{2,1,0:T(8,128)(2,1)} %qr_hbm.1, s32[4]{0:T(128)} %owners.1, ...), custom_call_target="tpu_custom_call" | custom-call | tf_op jit(solution)/shard_map/pallas_call | solution.py:413
  76.5 1.2 %copy.11 = f32[1,4]{1,0:T(1,128)} copy(f32[1,4]{1,0:T(1,128)} %shard_map.91) | data formatting | bytes 32
